TPU v7x, 512 devices: a whole 4x8x8 slice. The times are simulated.
512 devices in a mesh: gx: 8 (over y_lo, x), gy: 4 (over y_hi), gz: 16 (over z, core).
Axes of the slice: x: 4, y: 8 (y_hi: 4, y_lo: 2; y = y_hi * 2 + y_lo), z: 8, core: 2. Of those that a mesh axis runs over, the one named last changes fastest.
Arguments:
- source_term: float32 [64, 64, 2048], P('gx', 'gy', 'gz'), may hold values from -6 to 6
- conductivity: float32 [64, 64, 2048], P('gx', 'gy', 'gz'), may hold values from 0.3 to 3
- initial_guess: float32 [64, 64, 2048], P('gx', 'gy', 'gz'), may hold values from -4 to 4
- box_owner: int32 [8, 4, 16], replicated, may hold values from 0 to 3
Outputs:
- potential: float32 [64, 64, 2048], P('gx', 'gy', 'gz')
Inputs may be any that keep to these rules, and one draw needn't show every extreme that they name: `box_owner`: labels of the coarse boxes; boxes with equal labels couple only within one plane of boxes along z.
All inputs are finite; a program needn't handle non-finite values.
Results may differ from a plain program's by a relative error of at most 0.0001.
Values sent between devices are 32-bit elements; how exact they have to be, the bound alone decides.
A program may use at most 64 MiB of HBM per device.

v0:
```python
import jax
import jax.numpy as jnp
from jax import lax
from jax.sharding import PartitionSpec as P

CSWEEPS = 8
screening = 0.05


def with_halo(block, sides, width):
    for axis, dim in sides:
        count = lax.axis_size(axis)
        forward = [(i, i + 1) for i in range(count - 1)]
        forward.append((count - 1, 0))
        backward = [(target, source) for source, target in forward]
        low = lax.ppermute(
            lax.slice_in_dim(block, block.shape[dim] - width, None, axis=dim), axis, forward
        )
        high = lax.ppermute(lax.slice_in_dim(block, 0, width, axis=dim), axis, backward)
        block = jnp.concatenate([low, block, high], axis=dim)
    return block


def coarsen(values):
    extent = values.shape
    return values.reshape(extent[0] // 2, 2, extent[1] // 2, 2, extent[2] // 2, 2).mean(
        axis=(1, 3, 5)
    )


def refine(values):
    return jnp.repeat(jnp.repeat(jnp.repeat(values, 2, 0), 2, 1), 2, 2)


def trimmed(values, margin):
    return values[margin:-margin, margin:-margin, margin:-margin]


def weights_from(padded, stiffness):
    centre = padded[1:-1, 1:-1, 1:-1]
    weights = (
        (centre + padded[2:, 1:-1, 1:-1]) * 0.5,
        (centre + padded[:-2, 1:-1, 1:-1]) * 0.5,
        (centre + padded[1:-1, 2:, 1:-1]) * 0.5,
        (centre + padded[1:-1, :-2, 1:-1]) * 0.5,
        (centre + padded[1:-1, 1:-1, 2:]) * 0.5,
        (centre + padded[1:-1, 1:-1, :-2]) * 0.5,
    )
    diagonal = screening + stiffness * (
        weights[0] + weights[1] + weights[2] + weights[3] + weights[4] + weights[5]
    )
    return (weights, diagonal)


def neighbour_sum(padded, weights, margin):
    parts = [trimmed(values, margin) for values in weights]
    return (
        parts[0] * padded[2:, 1:-1, 1:-1]
        + parts[1] * padded[:-2, 1:-1, 1:-1]
        + parts[2] * padded[1:-1, 2:, 1:-1]
        + parts[3] * padded[1:-1, :-2, 1:-1]
        + parts[4] * padded[1:-1, 1:-1, 2:]
        + parts[5] * padded[1:-1, 1:-1, :-2]
    )


def relax_cells(padded, depth, level_data, colour):
    weights, diagonal, source_ext, parity_ext, stiffness = level_data
    margin = 2 - depth
    centre = padded[1:-1, 1:-1, 1:-1]
    nearby = neighbour_sum(padded, weights, margin)
    updated = (trimmed(source_ext, margin) + stiffness * nearby) / trimmed(diagonal, margin)
    return jnp.where(trimmed(parity_ext, margin) == colour, updated, centre)


def smooth(field, level_data):
    for colour in (0, 1):
        padded = with_halo(field, (("gx", 0), ("gy", 1), ("gz", 2)), 1)
        field = relax_cells(padded, 1, level_data, colour)
    return field


def level_setup(coef, source, stiffness):
    coef_ext = jnp.pad(with_halo(coef, (("gx", 0), ("gy", 1), ("gz", 2)), 1), 1)
    source_ext = jnp.pad(source, 1)
    weights, diagonal = weights_from(coef_ext, stiffness)
    extent = source.shape
    x_index = jnp.arange(extent[0] + 2, dtype=jnp.int32) + lax.axis_index("gx") * extent[0] - 1
    y_index = jnp.arange(extent[1] + 2, dtype=jnp.int32) + lax.axis_index("gy") * extent[1] - 1
    z_index = jnp.arange(extent[2] + 2, dtype=jnp.int32) + lax.axis_index("gz") * extent[2] - 1
    parity_ext = (x_index[:, None, None] + y_index[None, :, None] + z_index[None, None, :]) % 2
    return (weights, diagonal, source_ext, parity_ext, stiffness)


def beside_all(field, weights):
    return (
        weights[0] * jnp.roll(field, -1, 0)
        + weights[1] * jnp.roll(field, 1, 0)
        + weights[2] * jnp.roll(field, -1, 1)
        + weights[3] * jnp.roll(field, 1, 1)
        + weights[4] * jnp.roll(field, -1, 2)
        + weights[5] * jnp.roll(field, 1, 2)
    )


def coarse_solve(source, diagonal, weights, labels, box_depth, stiffness):
    extent = source.shape
    z_local = jnp.arange(extent[2], dtype=jnp.int32) % box_depth
    z_up = jnp.broadcast_to((z_local != box_depth - 1)[None, None, :], extent)
    z_down = jnp.broadcast_to((z_local != 0)[None, None, :], extent)
    masks = (
        labels == jnp.roll(labels, -1, 0),
        labels == jnp.roll(labels, 1, 0),
        labels == jnp.roll(labels, -1, 1),
        labels == jnp.roll(labels, 1, 1),
        z_up,
        z_down,
    )
    cut_weights = tuple((weights[index] * masks[index].astype(jnp.float32) for index in range(6)))
    x_index = jnp.arange(extent[0], dtype=jnp.int32)
    y_index = jnp.arange(extent[1], dtype=jnp.int32)
    z_index = jnp.arange(extent[2], dtype=jnp.int32)
    parity = (x_index[:, None, None] + y_index[None, :, None] + z_index[None, None, :]) % 2
    correction = jnp.zeros(extent, jnp.float32)
    for _ in range(CSWEEPS):
        for colour in (0, 1):
            updated = (source + stiffness * beside_all(correction, cut_weights)) / diagonal
            correction = jnp.where(parity == colour, updated, correction)
    return correction


def assemble(gathered, boxes_x, boxes_y, boxes_z, box_extent):
    width_x, width_y, width_z = box_extent
    blocks = gathered.reshape(boxes_x, boxes_y, boxes_z, 8, width_x, width_y, width_z)
    blocks = blocks.transpose(3, 0, 4, 1, 5, 2, 6)
    return blocks.reshape(8, boxes_x * width_x, boxes_y * width_y, boxes_z * width_z)


def local(source_term, conductivity, initial_guess, box_owner):
    field = initial_guess
    source = source_term
    coef = conductivity
    saved = []
    for coarse_step in range(3):
        stiffness = 0.25**coarse_step
        level_data = level_setup(coef, source, stiffness)
        if coarse_step > 0:
            field = jnp.zeros(source.shape, jnp.float32)
        field = smooth(field, level_data)
        padded = with_halo(field, (("gx", 0), ("gy", 1), ("gz", 2)), 1)
        nearby = neighbour_sum(padded, level_data[0], 1)
        residual = source - (trimmed(level_data[1], 1) * field - stiffness * nearby)
        saved.append((field, level_data))
        source = coarsen(residual)
        coef = coarsen(coef)
    stiffness = 0.25**3
    coef_ext = with_halo(coef, (("gx", 0), ("gy", 1), ("gz", 2)), 1)
    weights, diagonal = weights_from(coef_ext, stiffness)
    box_extent = source.shape
    payload = jnp.stack((source, diagonal) + weights).reshape(
        1, 8, box_extent[0] * box_extent[1] * box_extent[2]
    )
    boxes_x = lax.axis_size("gx")
    boxes_y = lax.axis_size("gy")
    plane_index = lax.axis_index("gz")
    gathered = lax.all_gather(payload, ("gx", "gy", "gz"), axis=0, tiled=True)
    fields = assemble(gathered, boxes_x, boxes_y, lax.axis_size("gz"), box_extent)
    z_start = plane_index * box_extent[2]
    labels = jnp.repeat(
        jnp.repeat(jnp.repeat(box_owner, box_extent[0], 0), box_extent[1], 1), box_extent[2], 2
    )
    correction_all = coarse_solve(
        fields[0],
        fields[1],
        tuple((fields[index] for index in range(2, 8))),
        labels,
        box_extent[2],
        stiffness,
    )
    starts = (lax.axis_index("gx") * box_extent[0], lax.axis_index("gy") * box_extent[1], z_start)
    correction = lax.dynamic_slice(correction_all, starts, box_extent)
    for coarse_step in (2, 1, 0):
        field, level_data = saved[coarse_step]
        field = smooth(field + refine(correction), level_data)
        correction = field
    return correction


def solution(mesh):
    return jax.shard_map(
        local,
        mesh=mesh,
        in_specs=(P("gx", "gy", "gz"), P("gx", "gy", "gz"), P("gx", "gy", "gz"), P()),
        out_specs=P("gx", "gy", "gz"),
        check_vma=False,
    )
```

profile of v0, /device:TPU:8, one launch (start us, length us, event | category | flops | bytes accessed | tf_op | source)
XLA Modules:
  0.0 1306.6 jit_solution(13660067413614063454)
XLA Ops:
  0.0 4.7 collective-permute-start.30
  6.6 6.3 reshape.307
  19.2 5.2 collective-permute-start.72
  49.8 6.0 collective-permute-start.6
  57.8 6.0 collective-permute-start.25
  65.8 6.0 collective-permute-start.1
  75.3 4.2 collective-permute-done.33
  85.8 4.3 collective-permute-start.26
  100.2 5.1 collective-permute-start.56
  112.2 5.3 collective-permute-start.8
  119.5 5.5 collective-permute-done.9
  150.7 4.1 collective-permute-start.15
  171.7 5.6 collective-permute-done.19
  179.6 4.4 collective-permute-start.21
  187.4 4.5 collective-permute-done.35
  196.4 4.8 collective-permute-start.51
  201.5 5.6 reshape.306
  219.9 4.3 collective-permute-start.39
  248.3 4.1 collective-permute-done.43
  252.4 6.0 collective-permute-start.45
  258.5 4.3 collective-permute-start.44
  311.0 4.8 collective-permute-start.69
  323.5 798.0 %all_gather.3 = f32[512,8,32]{2,1,0:T(8,128)S(1)} all-gather(f32[1,8,32]{2,1,0:T(8,128)S(1)} %stack.32), channel_id=1, replica_groups=mesh['gx'=8,'gy'=4,'gz'=16] {'gx','gy','gz'}, dimensions={0}, use_global_device_ids=true | all-gather | bytes 525312 | tf_op jit(solution)/shard_map/all_gather | solution.py:166
  1122.2 4.3 reshape.309
  1126.5 4.7 fusion.419
  1164.6 4.8 collective-permute-start.81
  1188.3 4.8 collective-permute-start.87
  1213.9 4.3 collective-permute-start.92
  1236.7 5.8 collective-permute-start.99
  1244.7 4.1 collective-permute-done.98
  1270.7 4.3 collective-permute-done.105
  1292.5 4.8 collective-permute-start.111
  (668 shorter events, 352.3 us)
Async XLA Ops:
  0.0 57.8 %collective-permute-start.30 = (f32[1,8,64]{2,1,0:T(8,128)S(1)}, f32[1,8,64]{2,1,0:T(8,128)S(1)}, u32[]{:S(2)}, u32[]{:S(2)}) collective-permute-start(f32[1,8,64]{2,1,0:T(8,128)S(1)} %broadcast.418), channel_id=1, source_target_pairs={{64,0},{128,64},{192,128},{256,192},{320,256},{384,320},{448,384},... | collective-permute-start | bytes 6152 | tf_op jit(solution)/shard_map/ppermute | solution.py:19
  4.7 59.1 %collective-permute-start.31 = (f32[1,8,64]{2,1,0:T(8,128)S(1)}, f32[1,8,64]{2,1,0:T(8,128)S(1)}, u32[]{:S(2)}, u32[]{:S(2)}) collective-permute-start(f32[1,8,64]{2,1,0:T(8,128)S(1)} %broadcast.418), channel_id=1, source_target_pairs={{0,64},{64,128},{128,192},{192,256},{256,320},{320,384},{384,448},... | collective-permute-start | bytes 6152 | tf_op jit(solution)/shard_map/ppermute | solution.py:16
  16.4 20.8 %collective-permute-start.73 = (f32[1,2,16]{2,1,0:T(2,128)S(1)}, f32[1,2,16]{2,1,0:T(2,128)S(1)}, u32[]{:S(2)}, u32[]{:S(2)}) collective-permute-start(f32[1,2,16]{2,1,0:T(2,128)S(1)} %multiply_bitcast_fusion), channel_id=1, source_target_pairs={{0,64},{64,128},{128,192},{192,256},{256,320},{320,384},{384,448},... | collective-permute-start | bytes 392 | tf_op jit(solution)/shard_map/ppermute | solution.py:16
  19.2 21.0 %collective-permute-start.72 = (f32[1,2,16]{2,1,0:T(2,128)S(1)}, f32[1,2,16]{2,1,0:T(2,128)S(1)}, u32[]{:S(2)}, u32[]{:S(2)}) collective-permute-start(f32[1,2,16]{2,1,0:T(2,128)S(1)} %multiply_bitcast_fusion), channel_id=1, source_target_pairs={{64,0},{128,64},{192,128},{256,192},{320,256},{384,320},{448,384},... | collective-permute-start | bytes 392 | tf_op jit(solution)/shard_map/ppermute | solution.py:19
  24.4 25.4 %collective-permute-start.54 = (f32[1,4,32]{2,1,0:T(4,128)S(1)}, f32[1,4,32]{2,1,0:T(4,128)S(1)}, u32[]{:S(2)}, u32[]{:S(2)}) collective-permute-start(f32[1,4,32]{2,1,0:T(4,128)S(1)} %broadcast.427), channel_id=1, source_target_pairs={{64,0},{128,64},{192,128},{256,192},{320,256},{384,320},{448,384},... | collective-permute-start | bytes 1544 | tf_op jit(solution)/shard_map/ppermute | solution.py:19
  43.1 12.7 collective-permute-start.55
  47.8 57.5 %collective-permute-start.7 = (f32[1,16,128]{2,1,0:T(8,128)S(1)}, f32[1,16,128]{2,1,0:T(8,128)S(1)}, u32[]{:S(2)}, u32[]{:S(2)}) collective-permute-start(f32[1,16,128]{2,1,0:T(8,128)S(1)} %get-tuple-element.272), channel_id=1, source_target_pairs={{0,64},{64,128},{128,192},{192,256},{256,320},{320,384},{384,448},... | collective-permute-start | bytes 24584 | tf_op jit(solution)/shard_map/ppermute | solution.py:16
  49.8 59.6 %collective-permute-start.6 = (f32[1,16,128]{2,1,0:T(8,128)S(1)}, f32[1,16,128]{2,1,0:T(8,128)S(1)}, u32[]{:S(2)}, u32[]{:S(2)}) collective-permute-start(f32[1,16,128]{2,1,0:T(8,128)S(1)} %get-tuple-element.271), channel_id=1, source_target_pairs={{64,0},{128,64},{192,128},{256,192},{320,256},{384,320},{448,384},... | collective-permute-start | bytes 24584 | tf_op jit(solution)/shard_map/ppermute | solution.py:19
  55.8 41.5 %collective-permute-start = (f32[1,16,128]{2,1,0:T(8,128)S(1)}, f32[1,16,128]{2,1,0:T(8,128)S(1)}, u32[]{:S(2)}, u32[]{:S(2)}) collective-permute-start(f32[1,16,128]{2,1,0:T(8,128)S(1)} %get-tuple-element.270), channel_id=1, source_target_pairs={{0,64},{64,128},{128,192},{192,256},{256,320},{320,384},{384,448},... | collective-permute-start | bytes 24584 | tf_op jit(solution)/shard_map/ppermute | solution.py:16
  57.8 8.0 collective-permute-start.25
  63.8 8.0 collective-permute-start.24
  65.8 34.4 %collective-permute-start.1 = (f32[1,16,128]{2,1,0:T(8,128)S(1)}, f32[1,16,128]{2,1,0:T(8,128)S(1)}, u32[]{:S(2)}, u32[]{:S(2)}) collective-permute-start(f32[1,16,128]{2,1,0:T(8,128)S(1)} %get-tuple-element.269), channel_id=1, source_target_pairs={{64,0},{128,64},{192,128},{256,192},{320,256},{384,320},{448,384},... | collective-permute-start | bytes 24584 | tf_op jit(solution)/shard_map/ppermute | solution.py:19
  93.4 185.7 %collective-permute-start.74 = (f32[3,1,16]{2,1,0:T(1,128)S(1)}, f32[3,1,16]{2,1,0:T(1,128)S(1)}, u32[]{:S(2)}, u32[]{:S(2)}) collective-permute-start(f32[3,1,16]{2,1,0:T(1,128)S(1)} %get-tuple-element.374), channel_id=1, source_target_pairs={{16,0},{32,16},{48,32},{0,48},{17,1},{33,17},{49,33},{1,49},{18,2}... | collective-permute-start | bytes 584 | tf_op jit(solution)/shard_map/ppermute | solution.py:19
  97.3 181.9 %collective-permute-start.75 = (f32[3,1,16]{2,1,0:T(1,128)S(1)}, f32[3,1,16]{2,1,0:T(1,128)S(1)}, u32[]{:S(2)}, u32[]{:S(2)}) collective-permute-start(f32[3,1,16]{2,1,0:T(1,128)S(1)} %get-tuple-element.373), channel_id=1, source_target_pairs={{0,16},{16,32},{32,48},{48,0},{1,17},{17,33},{33,49},{49,1},{2,18}... | collective-permute-start | bytes 584 | tf_op jit(solution)/shard_map/ppermute | solution.py:16
  100.2 110.2 %collective-permute-start.56 = (f32[4,1,32]{2,1,0:T(1,128)S(1)}, f32[4,1,32]{2,1,0:T(1,128)S(1)}, u32[]{:S(2)}, u32[]{:S(2)}) collective-permute-start(f32[4,1,32]{2,1,0:T(1,128)S(1)} %get-tuple-element.358), channel_id=1, source_target_pairs={{16,0},{32,16},{48,32},{0,48},{17,1},{33,17},{49,33},{1,49},{18,2}... | collective-permute-start | bytes 1544 | tf_op jit(solution)/shard_map/ppermute | solution.py:19
  109.4 8.0 collective-permute-start.2
  117.4 7.6 collective-permute-start.9
  125.2 10.3 collective-permute-start.11
  140.3 7.7 collective-permute-start.13
  169.6 7.7 collective-permute-start.19
  193.2 19.1 %collective-permute-start.57 = (f32[4,1,32]{2,1,0:T(1,128)S(1)}, f32[4,1,32]{2,1,0:T(1,128)S(1)}, u32[]{:S(2)}, u32[]{:S(2)}) collective-permute-start(f32[4,1,32]{2,1,0:T(1,128)S(1)} %get-tuple-element.357), channel_id=1, source_target_pairs={{0,16},{16,32},{32,48},{48,0},{1,17},{17,33},{33,49},{49,1},{2,18}... | collective-permute-start | bytes 1544 | tf_op jit(solution)/shard_map/ppermute | solution.py:16
  196.4 37.6 %collective-permute-start.51 = (f32[4,1,32]{2,1,0:T(1,128)S(1)}, f32[4,1,32]{2,1,0:T(1,128)S(1)}, u32[]{:S(2)}, u32[]{:S(2)}) collective-permute-start(f32[4,1,32]{2,1,0:T(1,128)S(1)} %get-tuple-element.356), channel_id=1, source_target_pairs={{16,0},{32,16},{48,32},{0,48},{17,1},{33,17},{49,33},{1,49},{18,2}... | collective-permute-start | bytes 1544 | tf_op jit(solution)/shard_map/ppermute | solution.py:19
  216.3 20.7 %collective-permute-start.50 = (f32[4,1,32]{2,1,0:T(1,128)S(1)}, f32[4,1,32]{2,1,0:T(1,128)S(1)}, u32[]{:S(2)}, u32[]{:S(2)}) collective-permute-start(f32[4,1,32]{2,1,0:T(1,128)S(1)} %get-tuple-element.355), channel_id=1, source_target_pairs={{0,16},{16,32},{32,48},{48,0},{1,17},{17,33},{33,49},{49,1},{2,18}... | collective-permute-start | bytes 1544 | tf_op jit(solution)/shard_map/ppermute | solution.py:16
  233.9 38.2 %collective-permute-start.59 = (f32[4,6,1]{2,1,0:T(8,128)S(1)}, f32[4,6,1]{2,1,0:T(8,128)S(1)}, u32[]{:S(2)}, u32[]{:S(2)}) collective-permute-start(f32[4,6,1]{2,1,0:T(8,128)S(1)} %get-tuple-element.342), channel_id=1, source_target_pairs={{0,1},{1,2},{2,3},{3,4},{4,5},{5,6},{6,7},{7,8},{8,9},{9,10},{10,1... | collective-permute-start | bytes 296 | tf_op jit(solution)/shard_map/ppermute | solution.py:16
  252.4 10.4 collective-permute-start.45
  282.8 8.2 collective-permute-start.62
  289.8 15.5 %collective-permute-start.76 = (f32[3,4,1]{2,1,0:T(4,128)S(1)}, f32[3,4,1]{2,1,0:T(4,128)S(1)}, u32[]{:S(2)}, u32[]{:S(2)}) collective-permute-start(f32[3,4,1]{2,1,0:T(4,128)S(1)} %get-tuple-element.360), channel_id=1, source_target_pairs={{1,0},{2,1},{3,2},{4,3},{5,4},{6,5},{7,6},{8,7},{9,8},{10,9},{11,1... | collective-permute-start | bytes 152 | tf_op jit(solution)/shard_map/ppermute | solution.py:19
  291.1 14.3 %collective-permute-start.77 = (f32[3,4,1]{2,1,0:T(4,128)S(1)}, f32[3,4,1]{2,1,0:T(4,128)S(1)}, u32[]{:S(2)}, u32[]{:S(2)}) collective-permute-start(f32[3,4,1]{2,1,0:T(4,128)S(1)} %get-tuple-element.359), channel_id=1, source_target_pairs={{0,1},{1,2},{2,3},{3,4},{4,5},{5,6},{6,7},{7,8},{8,9},{9,10},{10,1... | collective-permute-start | bytes 152 | tf_op jit(solution)/shard_map/ppermute | solution.py:16
  1210.3 8.0 collective-permute-start.93
  1236.7 8.0 collective-permute-start.99
  1256.3 7.7 collective-permute-start.103
  1282.9 7.7 collective-permute-start.109
  (145 other events, 4307.4 us)
where the time goes:
time: 1310 us
  blocking collectives  798 us (61%)
  starting transfers between devices  295 us (23%)
  waiting for transfers between devices  141 us (11%)
  local copies, waits for them, and re-layouts  49 us (4%)
  other arithmetic  20.4 us (2%)
    all_gather x1, blocking collectives, local(): gathered = lax.all_gather(payload, ('gx', 'gy', 'gz'), axis=0, tiled=True)  798 us
    ppermute x57, starting transfers between devices, with_halo(): lax.ppermute(lax.slice_in_dim(block, 0, width, axis=dim), axis, backward)  158 us
    ppermute x57, starting transfers between devices, with_halo(): lax.ppermute(lax.slice_in_dim(block, block.shape[dim] - width, None, axis...  137 us
    ppermute x57, waiting for transfers between devices, with_halo(): lax.ppermute(lax.slice_in_dim(block, block.shape[dim] - width, None, axis...  116 us
  transfers between devices with their start and end apart: 114, of which 51 were waited for; matrix products, arithmetic and copies ran while one was open for 3% of the time, Pallas kernels for 0%

commit v1 on v0

--- a/solution.py
+++ b/solution.py
@@ -163,7 +163,12 @@
     boxes_x = lax.axis_size("gx")
     boxes_y = lax.axis_size("gy")
     plane_index = lax.axis_index("gz")
-    gathered = lax.all_gather(payload, ("gx", "gy", "gz"), axis=0, tiled=True)
+    gathered = jnp.concatenate(
+        lax.all_to_all(
+            jnp.stack([payload] * lax.axis_size(("gx", "gy", "gz"))), ("gx", "gy", "gz"), 0, 0
+        ),
+        axis=0,
+    )
     fields = assemble(gathered, boxes_x, boxes_y, lax.axis_size("gz"), box_extent)
     z_start = plane_index * box_extent[2]
     labels = jnp.repeat(

time: 1310 us -> 547 us (0.42)
  blocking collectives: 798 us -> 0 us
  waiting for transfers between devices: 141 us -> 159 us
    all_gather x1 -> x0, blocking collectives: 798 us -> none  [local(): gathered = lax.all_gather(payload, ('gx', 'gy', 'gz'), axis=0, tiled=True)]
    all_to_all x0 -> x1, waiting for transfers between devices: none -> 17.1 us  [local(): lax.all_to_all(jnp.stack([payload] * lax.axis_size(('gx', 'gy', 'gz'))),...]
  transfers between devices with their start and end apart: 114 -> 115, of which waited for: 51 -> 52; matrix products, arithmetic and copies ran while one was open for 3% -> 6% of each run, Pallas kernels for 0% -> 0%
where the time goes in v1:
time: 547 us; the launch traced here: 544 us
  starting transfers between devices  308 us (56%)
  waiting for transfers between devices  159 us (29%)
  local copies, waits for them, and re-layouts  51.8 us (9%)
  other arithmetic  22.3 us (4%)
    ppermute x57, starting transfers between devices, with_halo(): lax.ppermute(lax.slice_in_dim(block, 0, width, axis=dim), axis, backward)  161 us
    ppermute x57, starting transfers between devices, with_halo(): lax.ppermute(lax.slice_in_dim(block, block.shape[dim] - width, None, axis...  134 us
    ppermute x57, waiting for transfers between devices, with_halo(): lax.ppermute(lax.slice_in_dim(block, block.shape[dim] - width, None, axis...  118 us
    ppermute x57, waiting for transfers between devices, with_halo(): lax.ppermute(lax.slice_in_dim(block, 0, width, axis=dim), axis, backward)  23.5 us
    all_to_all x1, waiting for transfers between devices, local(): lax.all_to_all(jnp.stack([payload] * lax.axis_size(('gx', 'gy', 'gz'))),...  17.1 us
    reshape x3, local copies, waits for them, and re-layouts, coarsen(): values.reshape(extent[0] // 2, 2, extent[1] // 2, 2, extent[2] // 2, 2)  12.5 us
    all_to_all x1, starting transfers between devices, local(): lax.all_to_all(jnp.stack([payload] * lax.axis_size(('gx', 'gy', 'gz'))),...  12.4 us
  transfers between devices with their start and end apart: 115, of which 52 were waited for; matrix products, arithmetic and copies ran while one was open for 6% of the time, Pallas kernels for 0%

profile of v1, /device:TPU:8, one launch (start us, length us, event | category | flops | bytes accessed | tf_op | source)
XLA Modules:
  0.0 544.3 jit_solution(15667286242418150591)
XLA Ops:
  0.0 4.7 collective-permute-start.30
  6.6 6.3 %reshape.306 = f32[4,2,8,2,64,2]{5,4,3,2,1,0:T(8,128)} reshape(f32[8,16,128]{2,1,0:T(8,128)} %param.5) | data formatting | bytes 131072 | tf_op jit(solution)/shard_map/reshape | solution.py:26
  19.2 5.2 collective-permute-start.72
  44.5 6.0 %collective-permute-start.6 = (f32[1,16,128]{2,1,0:T(8,128)S(1)}, f32[1,16,128]{2,1,0:T(8,128)S(1)}, u32[]{:S(2)}, u32[]{:S(2)}) collective-permute-start(f32[1,16,128]{2,1,0:T(8,128)S(1)} %get-tuple-element.271), channel_id=1, source_target_pairs={{64,0},{128,64},{192,128},{256,192},{320,256},{384,320},{448,384},... | collective-permute-start | bytes 24584 | tf_op jit(solution)/shard_map/ppermute | solution.py:19
  52.5 6.0 %collective-permute-start.25 = (f32[1,8,64]{2,1,0:T(8,128)S(1)}, f32[1,8,64]{2,1,0:T(8,128)S(1)}, u32[]{:S(2)}, u32[]{:S(2)}) collective-permute-start(f32[1,8,64]{2,1,0:T(8,128)S(1)} %get-tuple-element.346), channel_id=1, source_target_pairs={{64,0},{128,64},{192,128},{256,192},{320,256},{384,320},{448,384},... | collective-permute-start | bytes 6152 | tf_op jit(solution)/shard_map/ppermute | solution.py:19
  60.5 6.0 %collective-permute-start.1 = (f32[1,16,128]{2,1,0:T(8,128)S(1)}, f32[1,16,128]{2,1,0:T(8,128)S(1)}, u32[]{:S(2)}, u32[]{:S(2)}) collective-permute-start(f32[1,16,128]{2,1,0:T(8,128)S(1)} %get-tuple-element.269), channel_id=1, source_target_pairs={{64,0},{128,64},{192,128},{256,192},{320,256},{384,320},{448,384},... | collective-permute-start | bytes 24584 | tf_op jit(solution)/shard_map/ppermute | solution.py:19
  70.0 4.2 collective-permute-done.33
  80.6 4.3 collective-permute-start.26
  95.0 5.1 collective-permute-start.56
  106.9 5.3 collective-permute-start.8
  114.3 5.5 %collective-permute-done.9 = f32[10,1,128]{2,1,0:T(1,128)S(1)} collective-permute-done((f32[10,1,128]{2,1,0:T(1,128)S(1)}, f32[10,1,128]{2,1,0:T(1,128)S(1)}, u32[]{:S(2)}, u32[]{:S(2)}) %collective-permute-start.9) | collective-permute-done | bytes 5152 | tf_op jit(solution)/shard_map/ppermute | solution.py:16
  145.4 4.1 collective-permute-start.15
  166.4 5.6 %collective-permute-done.19 = f32[1,16,128]{2,1,0:T(8,128)S(1)} collective-permute-done((f32[1,16,128]{2,1,0:T(8,128)S(1)}, f32[1,16,128]{2,1,0:T(8,128)S(1)}, u32[]{:S(2)}, u32[]{:S(2)}) %collective-permute-start.19) | collective-permute-done | bytes 8224 | tf_op jit(solution)/shard_map/ppermute | solution.py:16
  174.4 4.4 collective-permute-start.21
  182.2 4.5 collective-permute-done.35
  191.1 4.8 collective-permute-start.51
  196.2 5.6 %reshape.305 = f32[4,2,8,2,64,2]{5,4,3,2,1,0:T(8,128)} reshape(f32[8,16,128]{2,1,0:T(8,128)S(1)} %fusion.44) | data formatting | bytes 131072 | tf_op jit(solution)/shard_map/reshape | solution.py:26
  214.6 4.3 collective-permute-start.39
  247.2 6.0 %collective-permute-start.45 = (f32[6,1,64]{2,1,0:T(1,128)S(1)}, f32[6,1,64]{2,1,0:T(1,128)S(1)}, u32[]{:S(2)}, u32[]{:S(2)}) collective-permute-start(f32[6,1,64]{2,1,0:T(1,128)S(1)} %get-tuple-element.307), channel_id=1, source_target_pairs={{0,16},{16,32},{32,48},{48,0},{1,17},{17,33},{33,49},{49,1},{2,18}... | collective-permute-start | bytes 4616 | tf_op jit(solution)/shard_map/ppermute | solution.py:16
  253.2 4.3 collective-permute-start.44
  305.7 5.0 collective-permute-start.69
  320.1 12.4 %all-to-all-start = ((f32[512,1,256]{2,1,0:T(1,128)}), f32[512,1,256]{2,1,0:T(1,128)S(1)}, u32[]{:S(2)}, u32[]{:S(2)}) async-start(f32[512,1,256]{2,1,0:T(1,128)} %reshape.316), calls=%async_computation | async-start | bytes 1048576 | tf_op jit(solution)/shard_map/all_to_all | solution.py:167
  337.7 17.1 %all-to-all-done = f32[512,1,256]{2,1,0:T(1,128)S(1)} async-done(((f32[512,1,256]{2,1,0:T(1,128)}), f32[512,1,256]{2,1,0:T(1,128)S(1)}, u32[]{:S(2)}, u32[]{:S(2)}) %all-to-all-start) | async-done | bytes 524320 | tf_op jit(solution)/shard_map/all_to_all | solution.py:167
  358.4 4.3 reshape_reshape.3
  362.7 4.7 fusion.419
  395.2 5.1 collective-permute-done.79
  402.4 4.6 collective-permute-start.81
  451.8 5.1 collective-permute-start.92
  474.4 5.8 %collective-permute-start.99 = (f32[6,1,64]{2,1,0:T(1,128)S(1)}, f32[6,1,64]{2,1,0:T(1,128)S(1)}, u32[]{:S(2)}, u32[]{:S(2)}) collective-permute-start(f32[6,1,64]{2,1,0:T(1,128)S(1)} %get-tuple-element.303), channel_id=1, source_target_pairs={{0,16},{16,32},{32,48},{48,0},{1,17},{17,33},{33,49},{49,1},{2,18}... | collective-permute-start | bytes 4616 | tf_op jit(solution)/shard_map/ppermute | solution.py:16
  482.4 4.1 collective-permute-done.98
  508.4 4.3 collective-permute-done.105
  530.2 4.8 collective-permute-start.111
  (674 shorter events, 361.3 us)
Async XLA Ops:
  0.0 52.5 %collective-permute-start.30 = (f32[1,8,64]{2,1,0:T(8,128)S(1)}, f32[1,8,64]{2,1,0:T(8,128)S(1)}, u32[]{:S(2)}, u32[]{:S(2)}) collective-permute-start(f32[1,8,64]{2,1,0:T(8,128)S(1)} %broadcast.420), channel_id=1, source_target_pairs={{64,0},{128,64},{192,128},{256,192},{320,256},{384,320},{448,384},... | collective-permute-start | bytes 6152 | tf_op jit(solution)/shard_map/ppermute | solution.py:19
  4.7 53.8 %collective-permute-start.31 = (f32[1,8,64]{2,1,0:T(8,128)S(1)}, f32[1,8,64]{2,1,0:T(8,128)S(1)}, u32[]{:S(2)}, u32[]{:S(2)}) collective-permute-start(f32[1,8,64]{2,1,0:T(8,128)S(1)} %broadcast.420), channel_id=1, source_target_pairs={{0,64},{64,128},{128,192},{192,256},{256,320},{320,384},{384,448},... | collective-permute-start | bytes 6152 | tf_op jit(solution)/shard_map/ppermute | solution.py:16
  16.4 15.5 %collective-permute-start.73 = (f32[1,2,16]{2,1,0:T(2,128)S(1)}, f32[1,2,16]{2,1,0:T(2,128)S(1)}, u32[]{:S(2)}, u32[]{:S(2)}) collective-permute-start(f32[1,2,16]{2,1,0:T(2,128)S(1)} %multiply_bitcast_fusion), channel_id=1, source_target_pairs={{0,64},{64,128},{128,192},{192,256},{256,320},{320,384},{384,448},... | collective-permute-start | bytes 392 | tf_op jit(solution)/shard_map/ppermute | solution.py:16
  19.2 15.8 %collective-permute-start.72 = (f32[1,2,16]{2,1,0:T(2,128)S(1)}, f32[1,2,16]{2,1,0:T(2,128)S(1)}, u32[]{:S(2)}, u32[]{:S(2)}) collective-permute-start(f32[1,2,16]{2,1,0:T(2,128)S(1)} %multiply_bitcast_fusion), channel_id=1, source_target_pairs={{64,0},{128,64},{192,128},{256,192},{320,256},{384,320},{448,384},... | collective-permute-start | bytes 392 | tf_op jit(solution)/shard_map/ppermute | solution.py:19
  24.4 20.1 %collective-permute-start.54 = (f32[1,4,32]{2,1,0:T(4,128)S(1)}, f32[1,4,32]{2,1,0:T(4,128)S(1)}, u32[]{:S(2)}, u32[]{:S(2)}) collective-permute-start(f32[1,4,32]{2,1,0:T(4,128)S(1)} %broadcast.429), channel_id=1, source_target_pairs={{64,0},{128,64},{192,128},{256,192},{320,256},{384,320},{448,384},... | collective-permute-start | bytes 1544 | tf_op jit(solution)/shard_map/ppermute | solution.py:19
  37.8 12.7 %collective-permute-start.55 = (f32[1,4,32]{2,1,0:T(4,128)S(1)}, f32[1,4,32]{2,1,0:T(4,128)S(1)}, u32[]{:S(2)}, u32[]{:S(2)}) collective-permute-start(f32[1,4,32]{2,1,0:T(4,128)S(1)} %broadcast.429), channel_id=1, source_target_pairs={{0,64},{64,128},{128,192},{192,256},{256,320},{320,384},{384,448},... | collective-permute-start | bytes 1544 | tf_op jit(solution)/shard_map/ppermute | solution.py:16
  42.5 57.5 %collective-permute-start.7 = (f32[1,16,128]{2,1,0:T(8,128)S(1)}, f32[1,16,128]{2,1,0:T(8,128)S(1)}, u32[]{:S(2)}, u32[]{:S(2)}) collective-permute-start(f32[1,16,128]{2,1,0:T(8,128)S(1)} %get-tuple-element.272), channel_id=1, source_target_pairs={{0,64},{64,128},{128,192},{192,256},{256,320},{320,384},{384,448},... | collective-permute-start | bytes 24584 | tf_op jit(solution)/shard_map/ppermute | solution.py:16
  44.5 59.6 %collective-permute-start.6 = (f32[1,16,128]{2,1,0:T(8,128)S(1)}, f32[1,16,128]{2,1,0:T(8,128)S(1)}, u32[]{:S(2)}, u32[]{:S(2)}) collective-permute-start(f32[1,16,128]{2,1,0:T(8,128)S(1)} %get-tuple-element.271), channel_id=1, source_target_pairs={{64,0},{128,64},{192,128},{256,192},{320,256},{384,320},{448,384},... | collective-permute-start | bytes 24584 | tf_op jit(solution)/shard_map/ppermute | solution.py:19
  50.5 41.5 %collective-permute-start = (f32[1,16,128]{2,1,0:T(8,128)S(1)}, f32[1,16,128]{2,1,0:T(8,128)S(1)}, u32[]{:S(2)}, u32[]{:S(2)}) collective-permute-start(f32[1,16,128]{2,1,0:T(8,128)S(1)} %get-tuple-element.270), channel_id=1, source_target_pairs={{0,64},{64,128},{128,192},{192,256},{256,320},{320,384},{384,448},... | collective-permute-start | bytes 24584 | tf_op jit(solution)/shard_map/ppermute | solution.py:16
  52.5 8.0 %collective-permute-start.25 = (f32[1,8,64]{2,1,0:T(8,128)S(1)}, f32[1,8,64]{2,1,0:T(8,128)S(1)}, u32[]{:S(2)}, u32[]{:S(2)}) collective-permute-start(f32[1,8,64]{2,1,0:T(8,128)S(1)} %get-tuple-element.346), channel_id=1, source_target_pairs={{64,0},{128,64},{192,128},{256,192},{320,256},{384,320},{448,384},... | collective-permute-start | bytes 6152 | tf_op jit(solution)/shard_map/ppermute | solution.py:19
  58.6 8.0 %collective-permute-start.24 = (f32[1,8,64]{2,1,0:T(8,128)S(1)}, f32[1,8,64]{2,1,0:T(8,128)S(1)}, u32[]{:S(2)}, u32[]{:S(2)}) collective-permute-start(f32[1,8,64]{2,1,0:T(8,128)S(1)} %get-tuple-element.345), channel_id=1, source_target_pairs={{0,64},{64,128},{128,192},{192,256},{256,320},{320,384},{384,448},... | collective-permute-start | bytes 6152 | tf_op jit(solution)/shard_map/ppermute | solution.py:16
  60.5 34.4 %collective-permute-start.1 = (f32[1,16,128]{2,1,0:T(8,128)S(1)}, f32[1,16,128]{2,1,0:T(8,128)S(1)}, u32[]{:S(2)}, u32[]{:S(2)}) collective-permute-start(f32[1,16,128]{2,1,0:T(8,128)S(1)} %get-tuple-element.269), channel_id=1, source_target_pairs={{64,0},{128,64},{192,128},{256,192},{320,256},{384,320},{448,384},... | collective-permute-start | bytes 24584 | tf_op jit(solution)/shard_map/ppermute | solution.py:19
  88.2 185.7 %collective-permute-start.74 = (f32[3,1,16]{2,1,0:T(1,128)S(1)}, f32[3,1,16]{2,1,0:T(1,128)S(1)}, u32[]{:S(2)}, u32[]{:S(2)}) collective-permute-start(f32[3,1,16]{2,1,0:T(1,128)S(1)} %get-tuple-element.374), channel_id=1, source_target_pairs={{16,0},{32,16},{48,32},{0,48},{17,1},{33,17},{49,33},{1,49},{18,2}... | collective-permute-start | bytes 584 | tf_op jit(solution)/shard_map/ppermute | solution.py:19
  92.0 181.9 %collective-permute-start.75 = (f32[3,1,16]{2,1,0:T(1,128)S(1)}, f32[3,1,16]{2,1,0:T(1,128)S(1)}, u32[]{:S(2)}, u32[]{:S(2)}) collective-permute-start(f32[3,1,16]{2,1,0:T(1,128)S(1)} %get-tuple-element.373), channel_id=1, source_target_pairs={{0,16},{16,32},{32,48},{48,0},{1,17},{17,33},{33,49},{49,1},{2,18}... | collective-permute-start | bytes 584 | tf_op jit(solution)/shard_map/ppermute | solution.py:16
  95.0 110.1 %collective-permute-start.56 = (f32[4,1,32]{2,1,0:T(1,128)S(1)}, f32[4,1,32]{2,1,0:T(1,128)S(1)}, u32[]{:S(2)}, u32[]{:S(2)}) collective-permute-start(f32[4,1,32]{2,1,0:T(1,128)S(1)} %get-tuple-element.358), channel_id=1, source_target_pairs={{16,0},{32,16},{48,32},{0,48},{17,1},{33,17},{49,33},{1,49},{18,2}... | collective-permute-start | bytes 1544 | tf_op jit(solution)/shard_map/ppermute | solution.py:19
  104.1 8.0 %collective-permute-start.2 = (f32[10,1,128]{2,1,0:T(1,128)S(1)}, f32[10,1,128]{2,1,0:T(1,128)S(1)}, u32[]{:S(2)}, u32[]{:S(2)}) collective-permute-start(f32[10,1,128]{2,1,0:T(1,128)S(1)} %get-tuple-element.73), channel_id=1, source_target_pairs={{0,16},{16,32},{32,48},{48,0},{1,17},{17,33},{33,49},{49,1},{2,18}... | collective-permute-start | bytes 15368 | tf_op jit(solution)/shard_map/ppermute | solution.py:16
  119.9 10.3 %collective-permute-start.11 = (f32[10,18,1]{2,1,0:T(8,128)S(1)}, f32[10,18,1]{2,1,0:T(8,128)S(1)}, u32[]{:S(2)}, u32[]{:S(2)}) collective-permute-start(f32[10,18,1]{2,1,0:T(8,128)S(1)} %get-tuple-element.64), channel_id=1, source_target_pairs={{0,1},{1,2},{2,3},{3,4},{4,5},{5,6},{6,7},{7,8},{8,9},{9,10},{10,1... | collective-permute-start | bytes 2168 | tf_op jit(solution)/shard_map/ppermute | solution.py:16
  135.0 7.7 %collective-permute-start.13 = (f32[1,16,128]{2,1,0:T(8,128)S(1)}, f32[1,16,128]{2,1,0:T(8,128)S(1)}, u32[]{:S(2)}, u32[]{:S(2)}) collective-permute-start(f32[1,16,128]{2,1,0:T(8,128)S(1)} %get-tuple-element.267), channel_id=1, source_target_pairs={{0,64},{64,128},{128,192},{192,256},{256,320},{320,384},{384,448},... | collective-permute-start | bytes 24584 | tf_op jit(solution)/shard_map/ppermute | solution.py:16
  164.4 7.7 %collective-permute-start.19 = (f32[1,16,128]{2,1,0:T(8,128)S(1)}, f32[1,16,128]{2,1,0:T(8,128)S(1)}, u32[]{:S(2)}, u32[]{:S(2)}) collective-permute-start(f32[1,16,128]{2,1,0:T(8,128)S(1)} %get-tuple-element.265), channel_id=1, source_target_pairs={{0,64},{64,128},{128,192},{192,256},{256,320},{320,384},{384,448},... | collective-permute-start | bytes 24584 | tf_op jit(solution)/shard_map/ppermute | solution.py:16
  187.9 19.1 %collective-permute-start.57 = (f32[4,1,32]{2,1,0:T(1,128)S(1)}, f32[4,1,32]{2,1,0:T(1,128)S(1)}, u32[]{:S(2)}, u32[]{:S(2)}) collective-permute-start(f32[4,1,32]{2,1,0:T(1,128)S(1)} %get-tuple-element.357), channel_id=1, source_target_pairs={{0,16},{16,32},{32,48},{48,0},{1,17},{17,33},{33,49},{49,1},{2,18}... | collective-permute-start | bytes 1544 | tf_op jit(solution)/shard_map/ppermute | solution.py:16
  191.1 37.6 %collective-permute-start.51 = (f32[4,1,32]{2,1,0:T(1,128)S(1)}, f32[4,1,32]{2,1,0:T(1,128)S(1)}, u32[]{:S(2)}, u32[]{:S(2)}) collective-permute-start(f32[4,1,32]{2,1,0:T(1,128)S(1)} %get-tuple-element.356), channel_id=1, source_target_pairs={{16,0},{32,16},{48,32},{0,48},{17,1},{33,17},{49,33},{1,49},{18,2}... | collective-permute-start | bytes 1544 | tf_op jit(solution)/shard_map/ppermute | solution.py:19
  211.0 20.7 %collective-permute-start.50 = (f32[4,1,32]{2,1,0:T(1,128)S(1)}, f32[4,1,32]{2,1,0:T(1,128)S(1)}, u32[]{:S(2)}, u32[]{:S(2)}) collective-permute-start(f32[4,1,32]{2,1,0:T(1,128)S(1)} %get-tuple-element.355), channel_id=1, source_target_pairs={{0,16},{16,32},{32,48},{48,0},{1,17},{17,33},{33,49},{49,1},{2,18}... | collective-permute-start | bytes 1544 | tf_op jit(solution)/shard_map/ppermute | solution.py:16
  228.6 38.2 %collective-permute-start.59 = (f32[4,6,1]{2,1,0:T(8,128)S(1)}, f32[4,6,1]{2,1,0:T(8,128)S(1)}, u32[]{:S(2)}, u32[]{:S(2)}) collective-permute-start(f32[4,6,1]{2,1,0:T(8,128)S(1)} %get-tuple-element.342), channel_id=1, source_target_pairs={{0,1},{1,2},{2,3},{3,4},{4,5},{5,6},{6,7},{7,8},{8,9},{9,10},{10,1... | collective-permute-start | bytes 296 | tf_op jit(solution)/shard_map/ppermute | solution.py:16
  247.2 10.4 %collective-permute-start.45 = (f32[6,1,64]{2,1,0:T(1,128)S(1)}, f32[6,1,64]{2,1,0:T(1,128)S(1)}, u32[]{:S(2)}, u32[]{:S(2)}) collective-permute-start(f32[6,1,64]{2,1,0:T(1,128)S(1)} %get-tuple-element.307), channel_id=1, source_target_pairs={{0,16},{16,32},{32,48},{48,0},{1,17},{17,33},{33,49},{49,1},{2,18}... | collective-permute-start | bytes 4616 | tf_op jit(solution)/shard_map/ppermute | solution.py:16
  277.5 8.1 %collective-permute-start.62 = (f32[4,1,32]{2,1,0:T(1,128)S(1)}, f32[4,1,32]{2,1,0:T(1,128)S(1)}, u32[]{:S(2)}, u32[]{:S(2)}) collective-permute-start(f32[4,1,32]{2,1,0:T(1,128)S(1)} %get-tuple-element.354), channel_id=1, source_target_pairs={{16,0},{32,16},{48,32},{0,48},{17,1},{33,17},{49,33},{1,49},{18,2}... | collective-permute-start | bytes 1544 | tf_op jit(solution)/shard_map/ppermute | solution.py:19
  284.4 15.7 %collective-permute-start.76 = (f32[3,4,1]{2,1,0:T(4,128)S(1)}, f32[3,4,1]{2,1,0:T(4,128)S(1)}, u32[]{:S(2)}, u32[]{:S(2)}) collective-permute-start(f32[3,4,1]{2,1,0:T(4,128)S(1)} %get-tuple-element.360), channel_id=1, source_target_pairs={{1,0},{2,1},{3,2},{4,3},{5,4},{6,5},{7,6},{8,7},{9,8},{10,9},{11,1... | collective-permute-start | bytes 152 | tf_op jit(solution)/shard_map/ppermute | solution.py:19
  285.6 14.5 %collective-permute-start.77 = (f32[3,4,1]{2,1,0:T(4,128)S(1)}, f32[3,4,1]{2,1,0:T(4,128)S(1)}, u32[]{:S(2)}, u32[]{:S(2)}) collective-permute-start(f32[3,4,1]{2,1,0:T(4,128)S(1)} %get-tuple-element.359), channel_id=1, source_target_pairs={{0,1},{1,2},{2,3},{3,4},{4,5},{5,6},{6,7},{7,8},{8,9},{9,10},{10,1... | collective-permute-start | bytes 152 | tf_op jit(solution)/shard_map/ppermute | solution.py:16
  320.1 34.7 %all-to-all-start = ((f32[512,1,256]{2,1,0:T(1,128)}), f32[512,1,256]{2,1,0:T(1,128)S(1)}, u32[]{:S(2)}, u32[]{:S(2)}) async-start(f32[512,1,256]{2,1,0:T(1,128)} %reshape.316), calls=%async_computation | async-start | bytes 1048576 | tf_op jit(solution)/shard_map/all_to_all | solution.py:167
  448.9 8.0 %collective-permute-start.93 = (f32[6,1,64]{2,1,0:T(1,128)S(1)}, f32[6,1,64]{2,1,0:T(1,128)S(1)}, u32[]{:S(2)}, u32[]{:S(2)}) collective-permute-start(f32[6,1,64]{2,1,0:T(1,128)S(1)} %get-tuple-element.305), channel_id=1, source_target_pairs={{0,16},{16,32},{32,48},{48,0},{1,17},{17,33},{33,49},{49,1},{2,18}... | collective-permute-start | bytes 4616 | tf_op jit(solution)/shard_map/ppermute | solution.py:16
  474.4 8.0 %collective-permute-start.99 = (f32[6,1,64]{2,1,0:T(1,128)S(1)}, f32[6,1,64]{2,1,0:T(1,128)S(1)}, u32[]{:S(2)}, u32[]{:S(2)}) collective-permute-start(f32[6,1,64]{2,1,0:T(1,128)S(1)} %get-tuple-element.303), channel_id=1, source_target_pairs={{0,16},{16,32},{32,48},{48,0},{1,17},{17,33},{33,49},{49,1},{2,18}... | collective-permute-start | bytes 4616 | tf_op jit(solution)/shard_map/ppermute | solution.py:16
  493.9 7.7 %collective-permute-start.103 = (f32[1,16,128]{2,1,0:T(8,128)S(1)}, f32[1,16,128]{2,1,0:T(8,128)S(1)}, u32[]{:S(2)}, u32[]{:S(2)}) collective-permute-start(f32[1,16,128]{2,1,0:T(8,128)S(1)} %get-tuple-element.79), channel_id=1, source_target_pairs={{0,64},{64,128},{128,192},{192,256},{256,320},{320,384},{384,448},... | collective-permute-start | bytes 24584 | tf_op jit(solution)/shard_map/ppermute | solution.py:16
  520.6 7.7 %collective-permute-start.109 = (f32[1,16,128]{2,1,0:T(8,128)S(1)}, f32[1,16,128]{2,1,0:T(8,128)S(1)}, u32[]{:S(2)}, u32[]{:S(2)}) collective-permute-start(f32[1,16,128]{2,1,0:T(8,128)S(1)} %get-tuple-element.77), channel_id=1, source_target_pairs={{0,64},{64,128},{128,192},{192,256},{256,320},{320,384},{384,448},... | collective-permute-start | bytes 24584 | tf_op jit(solution)/shard_map/ppermute | solution.py:16
  (146 other events, 4477.9 us)
